TPU v7x, 32 devices: a whole 2x2x4 slice. The times are simulated.
32 devices in a mesh: parts: 2 (over y), row: 8 (over z, x), col: 2 (over core).
Axes of the slice: x: 2, y: 2, z: 4, core: 2. Of those that a mesh axis runs over, the one named last changes fastest.
Arguments:
- queries: bfloat16 [16384, 256], P(('parts', 'row', 'col')), parts along dimension 0, may hold values from -6 to 6
- counts: int32 [32], P(('parts', 'row', 'col')), parts along dimension 0, may hold values from 1 to 512, as said below
- memory: bfloat16 [512, 256], P(('parts', 'row', 'col')), parts along dimension 0, may hold values from -6 to 6
- mem_mask: int32 [512], P(('parts', 'row', 'col')), parts along dimension 0, may hold values from 0 to 1, as said below
- cross_wq: bfloat16 [256, 256], replicated, may hold values from -0.375 to 0.375
- cross_wkv: bfloat16 [256, 512], replicated, may hold values from -0.375 to 0.375
- cross_wo: bfloat16 [256, 256], replicated, may hold values from -0.375 to 0.375
- self_wqkv: bfloat16 [256, 768], replicated, may hold values from -0.375 to 0.375
- self_wo: bfloat16 [256, 256], replicated, may hold values from -0.375 to 0.375
- ffn_up: bfloat16 [256, 2048], replicated, may hold values from -0.375 to 0.375
- ffn_down: bfloat16 [2048, 256], replicated, may hold values from -0.125 to 0.125
- box_w1: bfloat16 [256, 256], replicated, may hold values from -0.375 to 0.375
- box_w2: bfloat16 [256, 256], replicated, may hold values from -0.375 to 0.375
- box_w3: bfloat16 [256, 4], replicated, may hold values from -0.375 to 0.375
- cross_temp: float32 [8], replicated, may hold values from 1 to 100
- self_temp: float32 [8], replicated, may hold values from 1 to 100
Outputs:
- features: float32 [16384, 256], P(('parts', 'row', 'col')), parts along dimension 0
- boxes: float32 [4, 16384], P(None, ('parts', 'row', 'col')), parts along dimension 1
There are 2 independent parts, one for each index of `parts`. A program takes and returns all parts, laid end to end along the dimension named above; an argument that names none is the same for every part. Nothing has to cross between parts.
Inputs may be any that keep to these rules, and one draw needn't show every extreme that they name: The first counts[t] slots of tile t are live; some tile is full. `mem_mask`: the first memory token of every tile is live.
All inputs are finite; a program needn't handle non-finite values.
Results may differ from a plain program's by a relative error of at most 0.038.
The roundings to bfloat16 on the way count: a program that leaves them out, or rounds other values in their place, can miss the bound.
Values may be sent and summed in bfloat16 or wider, within the bound.
A program may use at most 64 MiB of HBM per device.

v0:
```python
import jax
import jax.numpy as jnp
from jax import lax
from jax.sharding import PartitionSpec as P

EPS = 1e-06


def rms_round(x):
    return (x * lax.rsqrt(jnp.mean(x * x, axis=-1, keepdims=True) + EPS)).astype(jnp.bfloat16)


def blend(state, q_block, keyval, live, scale):
    top_old, total_old, acc_old = state
    rows, heads, hsize = q_block.shape
    width = heads * hsize
    keys = keyval[:, :width].reshape(-1, heads, hsize)
    values = keyval[:, width:].reshape(-1, heads, hsize)
    scores = (
        jnp.einsum("qhd,khd->hqk", q_block, keys, preferred_element_type=jnp.float32)
        * scale[:, None, None]
    )
    keep = (live > 0)[None, None, :]
    top_new = jnp.maximum(top_old, jnp.max(jnp.where(keep, scores, -1e30), axis=-1))
    weights = jnp.where(keep, jnp.exp(scores - top_new[:, :, None]), 0.0)
    fade = jnp.exp(top_old - top_new)
    total_new = total_old * fade + jnp.sum(weights, axis=-1)
    mixed = jnp.einsum(
        "hqk,khd->qhd", weights.astype(jnp.bfloat16), values, preferred_element_type=jnp.float32
    )
    acc_new = acc_old * jnp.repeat(jnp.transpose(fade), hsize, axis=1) + mixed.reshape(rows, width)
    return (top_new, total_new, acc_new)


def sweep(state, q_all, keyval, live, scale, blocks, block):
    heads = scale.shape[0]
    hsize = q_all.shape[1] // heads

    def visit(index, carry):
        top, total, acc = carry
        begin = index * block
        q_block = lax.dynamic_slice_in_dim(q_all, begin, block, 0).reshape(block, heads, hsize)
        sub = (
            lax.dynamic_slice_in_dim(top, begin, block, 1),
            lax.dynamic_slice_in_dim(total, begin, block, 1),
            lax.dynamic_slice_in_dim(acc, begin, block, 0),
        )
        top_b, total_b, acc_b = blend(sub, q_block, keyval, live, scale)
        return (
            lax.dynamic_update_slice_in_dim(top, top_b, begin, 1),
            lax.dynamic_update_slice_in_dim(total, total_b, begin, 1),
            lax.dynamic_update_slice_in_dim(acc, acc_b, begin, 0),
        )

    return lax.fori_loop(0, blocks, visit, state)


def start_state(heads, rows, width):
    return (
        jnp.full((heads, rows), -1e30, jnp.float32),
        jnp.zeros((heads, rows), jnp.float32),
        jnp.zeros((rows, width), jnp.float32),
    )


def finish(state, valid, hsize):
    top, total, acc = state
    mixed = acc / jnp.repeat(jnp.transpose(total), hsize, axis=1)
    return jnp.where(valid[:, None], mixed, 0.0).astype(jnp.bfloat16)


def local(
    queries,
    counts,
    memory,
    mem_mask,
    cross_wq,
    cross_wkv,
    cross_wo,
    self_wqkv,
    self_wo,
    ffn_up,
    ffn_down,
    box_w1,
    box_w2,
    box_w3,
    cross_temp,
    self_temp,
):
    rows = queries.shape[0]
    width = queries.shape[1]
    heads = cross_temp.shape[0]
    hsize = width // heads
    block = min(128, rows)
    blocks = rows // block
    valid = jnp.arange(rows, dtype=jnp.int32) < counts[0]
    xres = queries.astype(jnp.float32)
    hn0 = rms_round(xres)
    qc = jnp.dot(hn0, cross_wq, preferred_element_type=jnp.float32).astype(jnp.bfloat16)
    scale_c = cross_temp / jnp.sqrt(jnp.float32(hsize))
    mask_flags = mem_mask.astype(jnp.bfloat16)
    initial = start_state(heads, rows, width)
    kvm = jnp.dot(memory, cross_wkv, preferred_element_type=jnp.float32).astype(jnp.bfloat16)
    piece = (
        lax.all_gather(kvm, "row", axis=0, tiled=True),
        lax.all_gather(mask_flags, "row", axis=0, tiled=True),
    )
    state = sweep(initial, qc, piece[0], piece[1], scale_c, blocks, block)
    ctx = finish(state, valid, hsize)
    x1 = xres + jnp.dot(ctx, cross_wo, preferred_element_type=jnp.float32)
    hn1 = rms_round(x1)
    qkv = jnp.dot(hn1, self_wqkv, preferred_element_type=jnp.float32).astype(jnp.bfloat16)
    q_self = qkv[:, :width]
    kv_self = qkv[:, width:]
    live_flags = valid.astype(jnp.bfloat16)
    scale_s = self_temp / jnp.sqrt(jnp.float32(hsize))
    piece = (
        lax.all_gather(kv_self, "col", axis=0, tiled=True),
        lax.all_gather(live_flags, "col", axis=0, tiled=True),
    )
    state_self = sweep(
        start_state(heads, rows, width), q_self, piece[0], piece[1], scale_s, blocks, block
    )
    sctx = finish(state_self, valid, hsize)
    x2 = x1 + jnp.dot(sctx, self_wo, preferred_element_type=jnp.float32)
    hn2 = rms_round(x2)
    upper = jnp.maximum(jnp.dot(hn2, ffn_up, preferred_element_type=jnp.float32), 0.0).astype(
        jnp.bfloat16
    )
    x3 = x2 + jnp.dot(upper, ffn_down, preferred_element_type=jnp.float32)
    features = jnp.where(valid[:, None], x3, 0.0)
    hn3 = rms_round(x3)
    b1 = jnp.maximum(jnp.dot(hn3, box_w1, preferred_element_type=jnp.float32), 0.0).astype(
        jnp.bfloat16
    )
    b2 = jnp.maximum(jnp.dot(b1, box_w2, preferred_element_type=jnp.float32), 0.0).astype(
        jnp.bfloat16
    )
    raw_box = jax.nn.sigmoid(jnp.dot(b2, box_w3, preferred_element_type=jnp.float32))
    boxes = jnp.transpose(jnp.where(valid[:, None], raw_box, 0.0))
    return (features, boxes)


def solution(mesh):
    return jax.shard_map(
        local,
        mesh=mesh,
        in_specs=(
            P(("parts", "row", "col"), None),
            P(("parts", "row", "col")),
            P(("parts", "row", "col"), None),
            P(("parts", "row", "col")),
            P(),
            P(),
            P(),
            P(),
            P(),
            P(),
            P(),
            P(),
            P(),
            P(),
            P(),
            P(),
        ),
        out_specs=(P(("parts", "row", "col"), None), P(None, ("parts", "row", "col"))),
        check_vma=False,
    )
```

profile of v0, /device:TPU:1, one launch (start us, length us, event | category | flops | bytes accessed | tf_op | source)
XLA Modules:
  0.0 117.1 jit_solution(806444376647798792)
XLA Ops:
  8.0 0.7 convert_element_type.60
  8.6 0.7 broadcast_multiply_fusion.1
  9.3 1.3 %dynamic-slice = u32[1]{0:T(128)} dynamic-slice(u32[32]{0:T(128)} %constant.132, u32[]{:T(128)S(6)} %add.140), dynamic_slice_sizes={1} | dynamic-slice | bytes 12
  11.3 0.2 dynamic-update-slice
  11.6 18.7 %all-reduce = bf16[128]{0:T(256)(128)(2,1)S(1)} all-reduce(bf16[128]{0:T(256)(128)(2,1)S(1)} %dynamic-update-slice), channel_id=1, replica_groups=mesh['parts'=2,'row'=8,'col'=2] {'row'}, use_global_device_ids=true, to_apply=%add | all-reduce | flops 128 | bytes 512
  30.3 1.1 convolution_convert_fusion.2
  31.4 24.2 %all_gather.13 = bf16[128,512]{1,0:T(8,128)(2,1)S(1)} all-gather(bf16[16,512]{1,0:T(8,128)(2,1)S(1)} %convolution_convert_fusion.2), channel_id=1, replica_groups=mesh['parts'=2,'row'=8,'col'=2] {'row'}, dimensions={0}, use_global_device_ids=true | all-gather | bytes 147456 | tf_op jit(solution)/shard_map/all_gather | solution.py:105
  55.6 0.1 copy.35
  55.7 1.1 copy.33
  56.9 1.2 %convolution_convert_fusion.1 = bf16[512,256]{1,0:T(8,128)(2,1)S(1)} fusion(bf16[256,256]{1,0:T(8,128)(2,1)} %param.24, bf16[512,256]{0,1:T(8,128)(2,1)S(1)} %copy.33, f32[512]{0:T(512)S(1)} %add_rsqrt_fusion.3), kind=kOutput, calls=%fused_computation.45 | convolution fusion | flops 67633152 | bytes 657408 | tf_op jit(solution)/shard_map/dot_general | solution.py:99
  58.2 3.8 %while.34 = (s32[]{:T(128)}, f32[8,512]{1,0:T(8,128)S(1)}, f32[8,512]{1,0:T(8,128)S(1)}, f32[512,256]{0,1:T(8,128)S(1)}, bf16[128]{0:T(256)(128)(2,1)S(1)}, /*in...) while((s32[]{:T(128)}, f32[8,512]{1,0:T(8,128)S(1)}, ...), condition=%wide.region_4.5_spmd, body=%wide.region_1.4_spmd.sunk | while | flops 18025604 | bytes 2880467 | solution.py:55
  58.2 0.1 copy.49
  58.4 0.3 select_reduce_fusion.4
  58.7 0.1 fusion.86
  58.8 0.3 fusion.87
  59.2 0.1 copy.49
  59.3 0.3 select_reduce_fusion.4
  59.6 0.1 fusion.86
  59.7 0.3 fusion.87
  60.2 0.3 select_reduce_fusion.4
  60.6 0.1 fusion.86
  60.7 0.3 fusion.87
  61.2 0.3 select_reduce_fusion.4
  61.5 0.1 fusion.86
  61.6 0.3 fusion.87
  62.1 0.3 multiply_reduce_fusion.2
  62.4 0.4 convolution_convert_fusion
  62.8 0.8 slice.37
  63.7 12.3 %all-gather = bf16[2,1,512]{2,1,0:T(2,128)(2,1)S(1)} all-gather(bf16[1,1,512]{2,1,0:T(2,128)(2,1)S(1)} %reshape.135), channel_id=1, replica_groups=mesh['parts'=2,'row'=8,'col'=2] {'col'}, dimensions={0}, use_global_device_ids=true | all-gather | bytes 3072 | tf_op jit(solution)/shard_map/all_gather | solution.py:119
  76.0 4.6 %all-gather.3.cloned.1.call-done = bf16[1024,512]{1,0:T(8,128)(2,1)} async-done(((bf16[512,512]{1,0:T(8,128)(2,1)}), bf16[1024,512]{1,0:T(8,128)(2,1)}) %all-gather.3.cloned.1.call-update) | async-done | bytes 1048592 | tf_op jit(solution)/shard_map/all_gather | solution.py:118
  80.6 1.5 %copy.37 = bf16[1024,512]{0,1:T(8,128)(2,1)S(1)} copy(bf16[1024,512]{1,0:T(8,128)(2,1)} %all-gather.3.cloned.1.call-done) | data formatting | bytes 2097152 | tf_op jit(solution)/shard_map/while | solution.py:55
  82.1 0.6 broadcast.104
  82.7 0.6 broadcast.105
  83.3 20.0 %while.35 = (s32[]{:T(128)}, f32[8,512]{1,0:T(8,128)}, f32[8,512]{1,0:T(8,128)}, f32[512,256]{0,1:T(8,128)S(1)}, bf16[1024]{0:T(1024)(128)(2,1)S(1)}, /*index=5*...) while((s32[]{:T(128)}, f32[8,512]{1,0:T(8,128)}, ...), condition=%wide.region_9.10_spmd, body=%wide.region_6.9_spmd.sunk | while | flops 145821696 | bytes 16779596 | solution.py:55
  83.4 0.1 copy.50
  83.6 0.8 select_reduce_fusion.5
  84.5 1.0 fusion.95
  85.4 1.0 fusion.94
  86.5 1.3 %add_dynamic-update-slice_fusion.5 = (f32[8,512]{1,0:T(8,128)}, f32[8,512]{1,0:T(8,128)S(1)}) fusion(f32[8,512]{1,0:T(8,128)} %get-tuple-element.575, s32[]{:T(128)S(6)} %select_n.115, f32[8,128]{1,0:T(8,128)S(1)} %fusion.94, f32[8,128]{1,0:T(8,128)S(1)} %get-tuple-element.520, f32[8,512]{1,0:T(8,128)S(1)} %copy-done.2), kind=kLoop, calls=%fused_computation.28.clone.1 | loop fusion | flops 3072 | bytes 24580 | tf_op jit(solution)/shard_map/while/body/eval_jaxpr/dynamic_update_slice | solution.py:51
  87.8 0.6 copy-done.3
  88.4 0.1 copy.50
  88.6 0.8 select_reduce_fusion.5
  89.5 1.0 fusion.95
  90.4 1.0 fusion.94
  91.5 1.3 %add_dynamic-update-slice_fusion.5 = (f32[8,512]{1,0:T(8,128)}, f32[8,512]{1,0:T(8,128)S(1)}) fusion(f32[8,512]{1,0:T(8,128)} %get-tuple-element.575, s32[]{:T(128)S(6)} %select_n.115, f32[8,128]{1,0:T(8,128)S(1)} %fusion.94, f32[8,128]{1,0:T(8,128)S(1)} %get-tuple-element.520, f32[8,512]{1,0:T(8,128)S(1)} %copy-done.2), kind=kLoop, calls=%fused_computation.28.clone.1 | loop fusion | flops 3072 | bytes 24580 | tf_op jit(solution)/shard_map/while/body/eval_jaxpr/dynamic_update_slice | solution.py:51
  92.8 0.6 copy-done.3
  93.4 0.1 copy.50
  93.6 0.8 select_reduce_fusion.5
  94.5 1.0 fusion.95
  95.4 1.0 fusion.94
  96.5 1.3 %add_dynamic-update-slice_fusion.5 = (f32[8,512]{1,0:T(8,128)}, f32[8,512]{1,0:T(8,128)S(1)}) fusion(f32[8,512]{1,0:T(8,128)} %get-tuple-element.575, s32[]{:T(128)S(6)} %select_n.115, f32[8,128]{1,0:T(8,128)S(1)} %fusion.94, f32[8,128]{1,0:T(8,128)S(1)} %get-tuple-element.520, f32[8,512]{1,0:T(8,128)S(1)} %copy-done.2), kind=kLoop, calls=%fused_computation.28.clone.1 | loop fusion | flops 3072 | bytes 24580 | tf_op jit(solution)/shard_map/while/body/eval_jaxpr/dynamic_update_slice | solution.py:51
  97.8 0.6 copy-done.3
  98.4 0.1 copy.50
  98.6 0.8 select_reduce_fusion.5
  99.5 1.0 fusion.95
  100.4 1.0 fusion.94
  101.5 1.3 %add_dynamic-update-slice_fusion.5 = (f32[8,512]{1,0:T(8,128)}, f32[8,512]{1,0:T(8,128)S(1)}) fusion(f32[8,512]{1,0:T(8,128)} %get-tuple-element.575, s32[]{:T(128)S(6)} %select_n.115, f32[8,128]{1,0:T(8,128)S(1)} %fusion.94, f32[8,128]{1,0:T(8,128)S(1)} %get-tuple-element.520, f32[8,512]{1,0:T(8,128)S(1)} %copy-done.2), kind=kLoop, calls=%fused_computation.28.clone.1 | loop fusion | flops 3072 | bytes 24580 | tf_op jit(solution)/shard_map/while/body/eval_jaxpr/dynamic_update_slice | solution.py:51
  102.8 0.6 copy-done.3
  103.3 0.8 fusion.28
  104.2 1.2 %multiply_reduce_fusion.1 = (f32[512]{0:T(512)S(1)}, f32[512,256]{0,1:T(8,128)S(1)}) fusion(f32[512,256]{0,1:T(8,128)S(1)} %get-tuple-element.391, bf16[512,256]{0,1:T(8,128)(2,1)S(1)} %fusion.28, bf16[256,256]{1,0:T(8,128)(2,1)} %param.28), kind=kOutput, calls=%fused_computation.68 | convolution fusion | flops 67501568 | bytes 1443840 | tf_op jit(solution)/shard_map/dot_general | solution.py:125
  105.4 2.5 %multiply_reduce_fusion = (f32[512]{0:T(512)S(1)}, f32[512,256]{0,1:T(8,128)S(1)}, f32[512,256]{0,1:T(8,128)S(1)}) fusion(pred[512]{0:T(512)(128)(4,1)S(1)} %iota_compare_fusion, f32[512,256]{0,1:T(8,128)S(1)} %get-tuple-element.393, bf16[2048,256]{1,0:T(8,128)(2,1)S(1)} %copy-done, bf16[256,2048]{1,0:T(8,128)(2,1)} %param.29, f32[512]{0:T(512)S(1)} %add_rsqrt_fusion.1), kind=kOutput, calls=%fused_computation.66 | convolution fusion | flops 1076624896 | bytes 3674624 | tf_op jit(solution)/shard_map/dot_general | solution.py:130
  108.0 1.0 copy.40
  109.0 0.5 fusion.19
  109.5 0.8 fusion.24
  (92 shorter events, 1.6 us)
Async XLA Ops:
  7.2 98.3 %copy-start = (bf16[2048,256]{1,0:T(8,128)(2,1)S(1)}, bf16[2048,256]{1,0:T(8,128)(2,1)}, u32[]{:S(2)}) copy-start(bf16[2048,256]{1,0:T(8,128)(2,1)} %param.30) | copy-start | bytes 3145732
  7.2 73.4 %all-gather.3.cloned.1.call-start = ((), (), s32[]{:S(2)}) async-start(), calls=%async_computation | async-start | bytes 1572864 | tf_op jit(solution)/shard_map/all_gather | solution.py:118
  58.1 3.9 %copy-start.4 = (bf16[256,256]{1,0:T(8,128)(2,1)S(1)}, bf16[256,256]{1,0:T(8,128)(2,1)}, u32[]{:S(2)}) copy-start(bf16[256,256]{1,0:T(8,128)(2,1)} %param.26) | copy-start | bytes 393220
  58.2 4.2 %copy-start.1 = (bf16[256,768]{1,0:T(8,128)(2,1)S(1)}, bf16[256,768]{1,0:T(8,128)(2,1)}, u32[]{:S(2)}) copy-start(bf16[256,768]{1,0:T(8,128)(2,1)} %param.27) | copy-start | bytes 1179652
  62.0 14.0 %copy-start.8 = (f32[8]{0:T(128)S(1)}, f32[8]{0:T(128)}, u32[]{:S(2)}) copy-start(f32[8]{0:T(128)} %param.35) | copy-start | bytes 100
  83.5 0.9 copy-start.2
  87.8 0.6 copy-start.3
  88.5 0.9 copy-start.2
  92.8 0.6 copy-start.3
  93.5 0.9 copy-start.2
  97.8 0.6 copy-start.3
  98.5 0.9 copy-start.2
  102.7 0.6 copy-start.3
  104.1 4.8 %copy-start.5 = (bf16[256,256]{1,0:T(8,128)(2,1)S(1)}, bf16[256,256]{1,0:T(8,128)(2,1)}, u32[]{:S(2)}) copy-start(bf16[256,256]{1,0:T(8,128)(2,1)} %param.32) | copy-start | bytes 393220
  104.1 4.8 %copy-start.6 = (bf16[256,256]{1,0:T(8,128)(2,1)S(1)}, bf16[256,256]{1,0:T(8,128)(2,1)}, u32[]{:S(2)}) copy-start(bf16[256,256]{1,0:T(8,128)(2,1)} %param.31) | copy-start | bytes 393220
  105.4 4.1 %copy-start.7 = (bf16[256,4]{0,1:T(4,128)(2,1)S(1)}, bf16[256,4]{0,1:T(4,128)(2,1)}, u32[]{:S(2)}) copy-start(bf16[256,4]{0,1:T(4,128)(2,1)} %param.33) | copy-start | bytes 6148
Sparse Core Ops, SparseCore 0:
  63.8 16.7 all-gather.2
where the time goes:
time: 118 us; the launch traced here: 117 us
  blocking collectives  55.1 us (47%)
  matrix products  17.4 us (15%)
  between operations  15.7 us (13%)
  other arithmetic  12.5 us (11%)
  local copies, waits for them, and re-layouts  11.1 us (9%)
  waiting for transfers between devices  4.61 us (4%)
    all_gather x1, blocking collectives, local(): lax.all_gather(kvm, 'row', axis=0, tiled=True)  24.2 us
    unnamed x1, blocking collectives  18.7 us
    all_gather x1, blocking collectives, local(): lax.all_gather(live_flags, 'col', axis=0, tiled=True)  12.3 us
    dynamic_update_slice x8, other arithmetic, visit(): lax.dynamic_update_slice_in_dim(total, total_b, begin, 1)  5.19 us
    dot_general x8, matrix products, blend(): jnp.einsum('hqk,khd->qhd', weights.astype(jnp.bfloat16), values, preferre...  4.9 us
    all_gather x1, waiting for transfers between devices, local(): lax.all_gather(kv_self, 'col', axis=0, tiled=True)  4.59 us
    reduce_sum x8, other arithmetic, blend(): total_new = total_old * fade + jnp.sum(weights, axis=-1)  4.58 us
    dot_general x8, matrix products, blend(): jnp.einsum('qhd,khd->hqk', q_block, keys, preferred_element_type=jnp.floa...  4.51 us
  transfers between devices with their start and end apart: 1, of which 1 were waited for; matrix products, arithmetic and copies ran while one was open for 0% of the time, Pallas kernels for 0%

commit v1 on v0

v1 whole, which is shorter than its diff:
```python
import functools
import math

import jax
import jax.numpy as jnp
from jax import lax
from jax.experimental import pallas as pl
from jax.experimental.pallas import tpu as pltpu
from jax.sharding import PartitionSpec as P

EPS = 1e-06
LANES = 128
BF = jnp.bfloat16
F32 = jnp.float32
MESH = pl.DeviceIdType.MESH


def rms_round(x):
    return (x * lax.rsqrt(jnp.mean(x * x, axis=-1, keepdims=True) + EPS)).astype(BF)


def mm(a, b):
    return jnp.dot(a, b, preferred_element_type=F32)


def each(n, body):
    if n <= 16:
        for i in range(n):
            body(i)
    else:
        lax.fori_loop(0, n, lambda i, c: (body(i), c)[1], 0)


def scale_row(temp_ref, width, hsize):
    head = lax.broadcasted_iota(jnp.int32, (1, width), 1) // hsize
    row = jnp.zeros((1, width), F32)
    for h in range(width // hsize):
        row = jnp.where(head == h, temp_ref[h], row)
    return row * (math.log2(math.e) / math.sqrt(hsize))


def attend(q, row, ka_ref, va_ref, hsize):
    rows, width = q.shape
    per = LANES // hsize
    qf = q.astype(F32) * row
    hi = qf.astype(BF).astype(F32)
    lo = qf - hi
    head = lax.broadcasted_iota(jnp.int32, (rows, LANES), 1) // hsize
    outs = []
    for g in range(width // LANES):
        lanes = slice(g * LANES, (g + 1) * LANES)
        lhs = jnp.concatenate(
            [
                jnp.concatenate(
                    [jnp.where(head == h, hi[:, lanes], 0.0), jnp.where(head == h, lo[:, lanes], 0.0)],
                    axis=1,
                ).astype(BF)
                for h in range(per)
            ],
            axis=0,
        )
        s = lax.dot_general(lhs, ka_ref[g], (((1,), (1,)), ((), ())), preferred_element_type=F32)
        e = jnp.exp2(s - jnp.max(s, axis=-1, keepdims=True)).astype(BF)
        o = mm(e, va_ref[g])
        num, den = o[:rows, :LANES], o[:rows, LANES:]
        for h in range(1, per):
            part = o[h * rows : (h + 1) * rows]
            num = jnp.where(head == h, part[:, :LANES], num)
            den = jnp.where(head == h, part[:, LANES:], den)
        outs.append(num / den)
    return jnp.concatenate(outs, axis=1)


def put_keys(ka_ref, va_ref, rows, k, v, live, first):
    flags = live.astype(F32).astype(BF)
    for g in range(k.shape[1] // LANES):
        lanes = slice(g * LANES, (g + 1) * LANES)
        kg = jnp.where(live, k[:, lanes], first[:, lanes]).astype(BF)
        ka_ref[g, rows, :LANES] = kg
        ka_ref[g, rows, LANES:] = kg
        va_ref[g, rows, :LANES] = jnp.where(live, v[:, lanes], 0.0).astype(BF)
        va_ref[g, rows, LANES:] = flags


def kernel(
    n_row, hsize, tm,
    q_hbm, cnt_s, mem_hbm, mask_s, wq_h, wkv_h, wo_h, wqkv_h, swo_h, up_h, down_h, w1_h, w2_h, w3_h,
    ct_s, st_s,
    feat_ref, box_ref,
    q_v, wq, wkv, wo, wqkv, swo, up, down, w1, w2, w3,
    gat, cnt, kac, vac, kas, vas, qc_v, x1_v, hn_v, hn_o, qs_v, sc_v,
    in_sem, gsend, grecv, csend, crecv, hsend, hrecv, msem,
):
    n, width = q_v.shape
    m_dev = mem_hbm.shape[0]
    row = lax.axis_index("row")
    other = 1 - lax.axis_index("col")

    barrier = pltpu.get_barrier_semaphore()

    def greet(i):
        pl.semaphore_signal(
            barrier, inc=1, device_id={"row": lax.rem(row + 1 + i, n_row)}, device_id_type=MESH
        )

    each(n_row - 1, greet)
    pl.semaphore_signal(barrier, inc=1, device_id={"col": other}, device_id_type=MESH)

    mine = pltpu.make_async_copy(mem_hbm, gat.at[row, :, pl.ds(0, width)], msem)
    mine.start()
    pairs = (
        (q_hbm, q_v), (wq_h, wq), (wkv_h, wkv), (wo_h, wo), (wqkv_h, wqkv),
        (swo_h, swo), (up_h, up), (down_h, down), (w1_h, w1), (w2_h, w2), (w3_h, w3),
    )
    loads = [pltpu.make_async_copy(a, b, in_sem.at[i]) for i, (a, b) in enumerate(pairs)]
    for load in loads:
        load.start()

    slot = lax.broadcasted_iota(jnp.int32, (m_dev, LANES), 0)
    flags = jnp.zeros((m_dev, LANES), jnp.int32)
    for i in range(m_dev):
        flags = jnp.where(slot == i, mask_s[i], flags)
    gat[row, :, pl.ds(width, LANES)] = (flags > 0).astype(F32).astype(BF)
    count = cnt_s[0]
    cnt[0] = jnp.full((8, LANES), count, jnp.int32)
    mine.wait()
    pl.semaphore_wait(barrier, n_row)

    def gather_copy(i):
        return pltpu.make_async_remote_copy(
            src_ref=gat.at[row], dst_ref=gat.at[row],
            send_sem=gsend.at[i], recv_sem=grecv.at[row],
            device_id={"row": lax.rem(row + 1 + i, n_row)}, device_id_type=MESH,
        )

    each(n_row - 1, lambda i: gather_copy(i).start())
    count_copy = pltpu.make_async_remote_copy(
        src_ref=cnt.at[0], dst_ref=cnt.at[1], send_sem=csend, recv_sem=crecv,
        device_id={"col": other}, device_id_type=MESH,
    )
    count_copy.start()

    loads[0].wait()
    loads[1].wait()
    qc_v[...] = mm(rms_round(q_v[...].astype(F32)), wq[...]).astype(BF)
    loads[2].wait()

    def arrived(i):
        j = lax.rem(row + 1 + i, n_row)
        pltpu.make_async_remote_copy(
            src_ref=gat.at[j], dst_ref=gat.at[j],
            send_sem=gsend.at[i], recv_sem=grecv.at[j],
            device_id={"row": j}, device_id_type=MESH,
        ).wait_recv()

    each(n_row - 1, arrived)

    keys = n_row * m_dev
    held = gat[...].reshape(keys, width + LANES)
    kv = mm(held[:, :width], wkv[...])
    live = held[:, width:].astype(F32) > 0.0
    put_keys(kac, vac, pl.ds(0, keys), kv[:, :width], kv[:, width:], live, kv[0:1, :width])

    cross_row = scale_row(ct_s, width, hsize)
    loads[3].wait()

    def hn_copy(t):
        rows = pl.ds(pl.multiple_of(t * tm, tm), tm)
        return pltpu.make_async_remote_copy(
            src_ref=hn_v.at[rows], dst_ref=hn_o.at[rows],
            send_sem=hsend.at[t], recv_sem=hrecv.at[t],
            device_id={"col": other}, device_id_type=MESH,
        )

    def cross_tile(t, carry):
        rows = pl.ds(pl.multiple_of(t * tm, tm), tm)
        ctx = attend(qc_v[rows, :], cross_row, kac, vac, hsize)
        alive = lax.broadcasted_iota(jnp.int32, (tm, width), 0) + t * tm < count
        ctx = jnp.where(alive, ctx, 0.0).astype(BF)
        x1 = q_v[rows, :].astype(F32) + mm(ctx, wo[...])
        x1_v[rows, :] = x1
        hn_v[rows, :] = rms_round(x1)
        hn_copy(t).start()
        return carry

    lax.fori_loop(0, n // tm, cross_tile, 0)

    loads[4].wait()
    qkv = mm(hn_v[...], wqkv[...])
    qs_v[...] = qkv[:, :width].astype(BF)
    k = qkv[:, width : 2 * width]
    first = k[0:1]
    spot = lax.broadcasted_iota(jnp.int32, (n, LANES), 0)
    put_keys(kas, vas, pl.ds(0, n), k, qkv[:, 2 * width :], spot < count, first)
    count_copy.wait()
    each(n // tm, lambda t: hn_copy(t).wait())
    kv_o = mm(hn_o[...], wqkv[:, width:])
    put_keys(kas, vas, pl.ds(n, n), kv_o[:, :width], kv_o[:, width:], spot < cnt[1, 0:1, :], first)

    self_row = scale_row(st_s, width, hsize)

    def self_tile(t, carry):
        rows = pl.ds(pl.multiple_of(t * tm, tm), tm)
        sctx = attend(qs_v[rows, :], self_row, kas, vas, hsize)
        alive = lax.broadcasted_iota(jnp.int32, (tm, width), 0) + t * tm < count
        sc_v[rows, :] = jnp.where(alive, sctx, 0.0).astype(BF)
        return carry

    lax.fori_loop(0, n // tm, self_tile, 0)

    for load in loads[5:]:
        load.wait()
    x2 = x1_v[...] + mm(sc_v[...], swo[...])
    hn2 = rms_round(x2)
    ff = up.shape[1]
    step = min(512, ff)
    x3 = x2
    for f in range(0, ff, step):
        upper = jnp.maximum(mm(hn2, up[:, f : f + step]), 0.0).astype(BF)
        x3 = x3 + mm(upper, down[f : f + step, :])
    alive = lax.broadcasted_iota(jnp.int32, (n, width), 0) < count
    feat_ref[...] = jnp.where(alive, x3, 0.0)
    hn3 = rms_round(x3)
    b1 = jnp.maximum(mm(hn3, w1[...]), 0.0).astype(BF)
    b2 = jnp.maximum(mm(b1, w2[...]), 0.0).astype(BF)
    z = lax.dot_general(w3[...], b2, (((0,), (1,)), ((), ())), preferred_element_type=F32)
    box = 1.0 / (1.0 + jnp.exp(-z))
    box_ref[...] = jnp.where(lax.broadcasted_iota(jnp.int32, box.shape, 1) < count, box, 0.0)

    each(n_row - 1, lambda i: gather_copy(i).wait_send())


def local(n_row, *args):
    queries, counts, memory, mem_mask = args[:4]
    weights = args[4:14]
    n, width = queries.shape
    m_dev = memory.shape[0]
    heads = args[14].shape[0]
    keys = n_row * m_dev
    groups = width // LANES
    tm = min(128, n)
    smem = pl.BlockSpec(memory_space=pltpu.SMEM)
    anyw = pl.BlockSpec(memory_space=pl.ANY)
    vmem = pl.BlockSpec(memory_space=pltpu.VMEM)
    dma = pltpu.SemaphoreType.DMA
    boxes = weights[-1].shape[1]
    return pl.pallas_call(
        functools.partial(kernel, n_row, width // heads, tm),
        out_shape=(
            jax.ShapeDtypeStruct((n, width), F32),
            jax.ShapeDtypeStruct((boxes, n), F32),
        ),
        in_specs=[anyw, smem, anyw, smem] + [anyw] * 10 + [smem, smem],
        out_specs=(vmem, vmem),
        scratch_shapes=[pltpu.VMEM(queries.shape, BF)]
        + [pltpu.VMEM(w.shape, BF) for w in weights]
        + [
            pltpu.VMEM((n_row, m_dev, width + LANES), BF),
            pltpu.VMEM((2, 8, LANES), jnp.int32),
            pltpu.VMEM((groups, keys, 2 * LANES), BF),
            pltpu.VMEM((groups, keys, 2 * LANES), BF),
            pltpu.VMEM((groups, 2 * n, 2 * LANES), BF),
            pltpu.VMEM((groups, 2 * n, 2 * LANES), BF),
            pltpu.VMEM((n, width), BF),
            pltpu.VMEM((n, width), F32),
            pltpu.VMEM((n, width), BF),
            pltpu.VMEM((n, width), BF),
            pltpu.VMEM((n, width), BF),
            pltpu.VMEM((n, width), BF),
            dma((11,)),
            dma((n_row - 1,)),
            dma((n_row,)),
            dma,
            dma,
            dma((n // tm,)),
            dma((n // tm,)),
            dma,
        ],
        compiler_params=pltpu.CompilerParams(
            collective_id=0, has_side_effects=True, vmem_limit_bytes=52 * 1024 * 1024
        ),
        name="spotter",
    )(*args)


def solution(mesh):
    spread = ("parts", "row", "col")
    return jax.shard_map(
        functools.partial(local, mesh.shape["row"]),
        mesh=mesh,
        in_specs=(P(spread, None), P(spread), P(spread, None), P(spread)) + (P(),) * 12,
        out_specs=(P(spread, None), P(None, spread)),
        check_vma=False,
    )
```

time: 118 us -> 38.4 us (0.33)
  blocking collectives: 55.1 us -> 0 us
  Pallas kernels: 0 us -> 25.8 us
  matrix products: 17.4 us -> 0 us
  between operations: 15.7 us -> 1.36 us
  other arithmetic: 12.5 us -> 0 us
  waiting for transfers between devices: 4.61 us -> 0 us
    all_gather x2 -> x0, blocking collectives: 36.4 us -> none  [the longest x1 24.2 us: local(): lax.all_gather(kvm, 'row', axis=0, tiled=True)]
    pallas_call x0 -> x1, Pallas kernels: none -> 25.8 us  [local(): pl.pallas_call(functools.partial(kernel, n_row, width // heads, tm), out_...]
    unnamed x1 -> x0, blocking collectives: 18.7 us -> none
    dot_general x24 -> x0, matrix products: 17.4 us -> none  [the longest x8 4.9 us: blend(): jnp.einsum('hqk,khd->qhd', weights.astype(jnp.bfloat16), values, preferre...]
    unnamed x21 -> x27, local copies, waits for them, and re-layouts: 3.72 us -> 10.7 us
    dynamic_update_slice x16 -> x0, other arithmetic: 5.48 us -> none  [the longest x8 5.19 us: visit(): lax.dynamic_update_slice_in_dim(total, total_b, begin, 1)]
    reduce_sum x9 -> x0, other arithmetic: 4.66 us -> none  [the longest x8 4.58 us: blend(): total_new = total_old * fade + jnp.sum(weights, axis=-1)]
    all_gather x1 -> x0, waiting for transfers between devices: 4.59 us -> none  [local(): lax.all_gather(kv_self, 'col', axis=0, tiled=True)]
  transfers between devices with their start and end apart: 1 -> 0, of which waited for: 1 -> 0; matrix products, arithmetic and copies ran while one was open for 0% -> 0% of each run, Pallas kernels for 0% -> 0%
where the time goes in v1:
time: 38.4 us; the launch traced here: 37.9 us
  Pallas kernels  25.8 us (67%)
  local copies, waits for them, and re-layouts  10.7 us (28%)
  between operations  1.36 us (4%)
    pallas_call x1, Pallas kernels, local(): pl.pallas_call(functools.partial(kernel, n_row, width // heads, tm), out_...  25.8 us
    unnamed x27, local copies, waits for them, and re-layouts  10.7 us

profile of v1, /device:TPU:1, one launch (start us, length us, event | category | flops | bytes accessed | tf_op | source)
XLA Modules:
  0.0 37.9 jit_solution(16005055368269732836)
XLA Ops:
  1.3 0.0 copy-start.8
  1.3 0.0 copy-start.9
  1.3 0.0 copy-start.10
  1.3 0.0 copy-start.11
  1.3 0.8 %copy.18.w3_h = bf16[256,4]{1,0:T(8,128)(2,1)S(1)} copy(bf16[256,4]{0,1:T(4,128)(2,1)} %param.29) | data formatting | bytes 4096 | tf_op args[13]
  2.2 0.0 copy-done.8
  2.2 0.0 copy-done.9
  2.2 0.0 copy-done.10
  2.2 0.0 copy-done.11
  2.2 0.0 copy-start
  2.2 1.0 %copy-done = bf16[256,768]{1,0:T(8,128)(2,1)S(1)} copy-done((bf16[256,768]{1,0:T(8,128)(2,1)S(1)}, bf16[256,768]{1,0:T(8,128)(2,1)}, u32[]{:S(2)}) %copy-start) | copy-done | bytes 393240
  3.2 0.0 copy-start.1
  3.2 0.9 %copy-done.1 = bf16[512,256]{1,0:T(8,128)(2,1)S(1)} copy-done((bf16[512,256]{1,0:T(8,128)(2,1)S(1)}, bf16[512,256]{1,0:T(8,128)(2,1)}, u32[]{:S(2)}) %copy-start.1) | copy-done | bytes 262168
  4.1 0.0 copy-start.2
  4.1 0.9 %copy-done.2 = bf16[256,512]{1,0:T(8,128)(2,1)S(1)} copy-done((bf16[256,512]{1,0:T(8,128)(2,1)S(1)}, bf16[256,512]{1,0:T(8,128)(2,1)}, u32[]{:S(2)}) %copy-start.2) | copy-done | bytes 262168
  5.1 0.0 copy-start.3
  5.1 0.9 %copy-done.3 = bf16[256,256]{1,0:T(8,128)(2,1)S(1)} copy-done((bf16[256,256]{1,0:T(8,128)(2,1)S(1)}, bf16[256,256]{1,0:T(8,128)(2,1)}, u32[]{:S(2)}) %copy-start.3) | copy-done | bytes 131096
  6.0 0.0 copy-start.4
  6.0 0.9 %copy-done.4 = bf16[256,256]{1,0:T(8,128)(2,1)S(1)} copy-done((bf16[256,256]{1,0:T(8,128)(2,1)S(1)}, bf16[256,256]{1,0:T(8,128)(2,1)}, u32[]{:S(2)}) %copy-start.4) | copy-done | bytes 131096
  6.9 0.0 copy-start.5
  6.9 0.9 %copy-done.5 = bf16[256,256]{1,0:T(8,128)(2,1)S(1)} copy-done((bf16[256,256]{1,0:T(8,128)(2,1)S(1)}, bf16[256,256]{1,0:T(8,128)(2,1)}, u32[]{:S(2)}) %copy-start.5) | copy-done | bytes 131096
  7.8 0.0 copy-start.6
  7.8 0.9 %copy-done.6 = bf16[256,256]{1,0:T(8,128)(2,1)S(1)} copy-done((bf16[256,256]{1,0:T(8,128)(2,1)S(1)}, bf16[256,256]{1,0:T(8,128)(2,1)}, u32[]{:S(2)}) %copy-start.6) | copy-done | bytes 131096
  8.7 0.0 copy-start.7
  8.7 0.9 %copy-done.7 = bf16[256,256]{1,0:T(8,128)(2,1)S(1)} copy-done((bf16[256,256]{1,0:T(8,128)(2,1)S(1)}, bf16[256,256]{1,0:T(8,128)(2,1)}, u32[]{:S(2)}) %copy-start.7) | copy-done | bytes 131096
  9.6 25.8 %spotter.1 = (f32[512,256]{1,0:T(8,128)}, f32[4,512]{1,0:T(4,128)S(1)}) custom-call(bf16[512,256]{1,0:T(8,128)(2,1)S(1)} %copy-done.1, s32[1]{0:T(128)S(6)} %copy.21.cnt_s, bf16[16,256]{1,0:T(8,128)(2,1)S(1)} %copy-done.8, s32[16]{0:T(128)S(1)} %copy-done.9, bf16[256,256]{1,0:T(8,128)(2,1)S(1)} %copy-done.3, bf16[256,512]{1,0:T(8,128)(2,1)S(1)} %copy-done.2, ...), custom_call_target="tpu_custom_call" | custom-call | tf_op jit(solution)/shard_map/spotter/pallas_call | solution.py:247
  35.4 1.9 %copy.22 = f32[512,256]{1,0:T(8,128)} copy(f32[512,256]{1,0:T(8,128)} %get-tuple-element.4) | data formatting | bytes 1048576
  37.3 0.6 %copy.23 = f32[4,512]{1,0:T(4,128)} copy(f32[4,512]{1,0:T(4,128)S(1)} %get-tuple-element.5) | data formatting | bytes 16384
Async XLA Ops:
  1.3 0.9 %copy-start.8 = (bf16[16,256]{1,0:T(8,128)(2,1)S(1)}, bf16[16,256]{1,0:T(8,128)(2,1)}, u32[]{:S(2)}) copy-start(bf16[16,256]{1,0:T(8,128)(2,1)} %mem_hbm.1) | copy-start | bytes 24580
  1.3 0.9 %copy-start.9 = (s32[16]{0:T(128)S(1)}, s32[16]{0:T(128)}, u32[]{:S(2)}) copy-start(s32[16]{0:T(128)} %mask_s.1) | copy-start | bytes 196
  1.3 0.9 %copy-start.10 = (f32[8]{0:T(128)S(1)}, f32[8]{0:T(128)}, u32[]{:S(2)}) copy-start(f32[8]{0:T(128)} %ct_s.1) | copy-start | bytes 100
  1.3 0.9 %copy-start.11 = (f32[8]{0:T(128)S(1)}, f32[8]{0:T(128)}, u32[]{:S(2)}) copy-start(f32[8]{0:T(128)} %st_s.1) | copy-start | bytes 100
  2.2 1.0 %copy-start = (bf16[256,768]{1,0:T(8,128)(2,1)S(1)}, bf16[256,768]{1,0:T(8,128)(2,1)}, u32[]{:S(2)}) copy-start(bf16[256,768]{1,0:T(8,128)(2,1)} %wqkv_h.1) | copy-start | bytes 1179652
  3.2 0.9 %copy-start.1 = (bf16[512,256]{1,0:T(8,128)(2,1)S(1)}, bf16[512,256]{1,0:T(8,128)(2,1)}, u32[]{:S(2)}) copy-start(bf16[512,256]{1,0:T(8,128)(2,1)} %q_hbm.1) | copy-start | bytes 786436
  4.1 0.9 %copy-start.2 = (bf16[256,512]{1,0:T(8,128)(2,1)S(1)}, bf16[256,512]{1,0:T(8,128)(2,1)}, u32[]{:S(2)}) copy-start(bf16[256,512]{1,0:T(8,128)(2,1)} %wkv_h.1) | copy-start | bytes 786436
  5.1 0.9 %copy-start.3 = (bf16[256,256]{1,0:T(8,128)(2,1)S(1)}, bf16[256,256]{1,0:T(8,128)(2,1)}, u32[]{:S(2)}) copy-start(bf16[256,256]{1,0:T(8,128)(2,1)} %wq_h.1) | copy-start | bytes 393220
  6.0 0.9 %copy-start.4 = (bf16[256,256]{1,0:T(8,128)(2,1)S(1)}, bf16[256,256]{1,0:T(8,128)(2,1)}, u32[]{:S(2)}) copy-start(bf16[256,256]{1,0:T(8,128)(2,1)} %wo_h.1) | copy-start | bytes 393220
  6.9 0.9 %copy-start.5 = (bf16[256,256]{1,0:T(8,128)(2,1)S(1)}, bf16[256,256]{1,0:T(8,128)(2,1)}, u32[]{:S(2)}) copy-start(bf16[256,256]{1,0:T(8,128)(2,1)} %swo_h.1) | copy-start | bytes 393220
  7.8 0.9 %copy-start.6 = (bf16[256,256]{1,0:T(8,128)(2,1)S(1)}, bf16[256,256]{1,0:T(8,128)(2,1)}, u32[]{:S(2)}) copy-start(bf16[256,256]{1,0:T(8,128)(2,1)} %w1_h.1) | copy-start | bytes 393220
  8.7 0.9 %copy-start.7 = (bf16[256,256]{1,0:T(8,128)(2,1)S(1)}, bf16[256,256]{1,0:T(8,128)(2,1)}, u32[]{:S(2)}) copy-start(bf16[256,256]{1,0:T(8,128)(2,1)} %w2_h.1) | copy-start | bytes 393220

commit v2 on v1

--- a/solution.py
+++ b/solution.py
@@ -223,16 +223,20 @@
     hn3 = rms_round(x3)
     b1 = jnp.maximum(mm(hn3, w1[...]), 0.0).astype(BF)
     b2 = jnp.maximum(mm(b1, w2[...]), 0.0).astype(BF)
-    z = lax.dot_general(w3[...], b2, (((0,), (1,)), ((), ())), preferred_element_type=F32)
+    z = lax.dot_general(w3[...], b2, (((1,), (1,)), ((), ())), preferred_element_type=F32)
     box = 1.0 / (1.0 + jnp.exp(-z))
     box_ref[...] = jnp.where(lax.broadcasted_iota(jnp.int32, box.shape, 1) < count, box, 0.0)
 
     each(n_row - 1, lambda i: gather_copy(i).wait_send())
 
 
+def pin(x):
+    return pltpu.with_memory_space_constraint(x, pltpu.HBM)
+
+
 def local(n_row, *args):
     queries, counts, memory, mem_mask = args[:4]
-    weights = args[4:14]
+    weights = args[4:13] + (args[13].T,)
     n, width = queries.shape
     m_dev = memory.shape[0]
     heads = args[14].shape[0]
@@ -240,17 +244,17 @@
     groups = width // LANES
     tm = min(128, n)
     smem = pl.BlockSpec(memory_space=pltpu.SMEM)
-    anyw = pl.BlockSpec(memory_space=pl.ANY)
+    hbm = pl.BlockSpec(memory_space=pltpu.HBM)
     vmem = pl.BlockSpec(memory_space=pltpu.VMEM)
     dma = pltpu.SemaphoreType.DMA
-    boxes = weights[-1].shape[1]
+    boxes = weights[-1].shape[0]
     return pl.pallas_call(
         functools.partial(kernel, n_row, width // heads, tm),
         out_shape=(
             jax.ShapeDtypeStruct((n, width), F32),
             jax.ShapeDtypeStruct((boxes, n), F32),
         ),
-        in_specs=[anyw, smem, anyw, smem] + [anyw] * 10 + [smem, smem],
+        in_specs=[hbm, smem, hbm, smem] + [hbm] * 10 + [smem, smem],
         out_specs=(vmem, vmem),
         scratch_shapes=[pltpu.VMEM(queries.shape, BF)]
         + [pltpu.VMEM(w.shape, BF) for w in weights]
@@ -280,7 +284,7 @@
             collective_id=0, has_side_effects=True, vmem_limit_bytes=52 * 1024 * 1024
         ),
         name="spotter",
-    )(*args)
+    )(pin(queries), counts, pin(memory), mem_mask, *map(pin, weights), *args[14:])
 
 
 def solution(mesh):

time: 38.4 us -> 29.3 us (0.76)
  local copies, waits for them, and re-layouts: 10.7 us -> 2.06 us
    unnamed x27 -> x8, local copies, waits for them, and re-layouts: 10.7 us -> 2.06 us
where the time goes in v2:
time: 29.3 us; the launch traced here: 29 us
  Pallas kernels  25.7 us (88%)
  local copies, waits for them, and re-layouts  2.06 us (7%)
  between operations  1.32 us (5%)
    pallas_call x1, Pallas kernels, local(): pl.pallas_call(functools.partial(kernel, n_row, width // heads, tm), out_...  25.7 us
    unnamed x8, local copies, waits for them, and re-layouts  2.06 us

profile of v2, /device:TPU:1, one launch (start us, length us, event | category | flops | bytes accessed | tf_op | source)
XLA Modules:
  0.0 29.0 jit_solution(3209749906316724172)
XLA Ops:
  1.3 0.0 copy-start
  1.3 0.0 copy-start.1
  1.3 0.0 copy-start.2
  1.3 0.6 %copy-done = s32[16]{0:T(128)S(1)} copy-done((s32[16]{0:T(128)S(1)}, s32[16]{0:T(128)}, u32[]{:S(2)}) %copy-start) | copy-done | bytes 88
  1.9 0.0 copy-done.1
  2.0 0.0 copy-done.2
  2.0 25.7 %spotter.1 = (f32[512,256]{1,0:T(8,128)S(1)}, f32[4,512]{1,0:T(4,128)S(1)}) custom-call(bf16[512,256]{1,0:T(8,128)(2,1)} %q_hbm.1, s32[1]{0:T(128)S(6)} %copy.20.cnt_s, bf16[16,256]{1,0:T(8,128)(2,1)} %mem_hbm.1, s32[16]{0:T(128)S(1)} %copy-done, bf16[256,256]{1,0:T(8,128)(2,1)} %wq_h.1, bf16[256,512]{1,0:T(8,128)(2,1)} %wkv_h.1, bf16[256,256]{1,0:T(8,128)(2,1)} %wo_h.1, ...), custom_call_target="tpu_custom_call" | custom-call | tf_op jit(solution)/shard_map/spotter/pallas_call | solution.py:251
  27.6 0.8 %copy.21 = f32[512,256]{1,0:T(8,128)} copy(f32[512,256]{1,0:T(8,128)S(1)} %get-tuple-element.4) | data formatting | bytes 1048576
  28.4 0.6 %copy.22 = f32[4,512]{1,0:T(4,128)} copy(f32[4,512]{1,0:T(4,128)S(1)} %get-tuple-element.5) | data formatting | bytes 16384
Async XLA Ops:
  1.3 0.7 %copy-start = (s32[16]{0:T(128)S(1)}, s32[16]{0:T(128)}, u32[]{:S(2)}) copy-start(s32[16]{0:T(128)} %mask_s.1) | copy-start | bytes 196
  1.3 0.7 %copy-start.1 = (f32[8]{0:T(128)S(1)}, f32[8]{0:T(128)}, u32[]{:S(2)}) copy-start(f32[8]{0:T(128)} %ct_s.1) | copy-start | bytes 100
  1.3 0.7 %copy-start.2 = (f32[8]{0:T(128)S(1)}, f32[8]{0:T(128)}, u32[]{:S(2)}) copy-start(f32[8]{0:T(128)} %st_s.1) | copy-start | bytes 100

commit v3 on v2

--- a/solution.py
+++ b/solution.py
@@ -13,6 +13,7 @@
 BF = jnp.bfloat16
 F32 = jnp.float32
 MESH = pl.DeviceIdType.MESH
+DEAD = 64.0
 
 
 def rms_round(x):
@@ -84,11 +85,11 @@
 
 def kernel(
     n_row, hsize, tm,
-    q_hbm, cnt_s, mem_hbm, mask_s, wq_h, wkv_h, wo_h, wqkv_h, swo_h, up_h, down_h, w1_h, w2_h, w3_h,
-    ct_s, st_s,
+    q_hbm, cnt_s, mem_hbm, mask_h, wq_h, wkv_h, wo_h, wqkv_h, swo_h, up_h, down_h, w1_h, w2_h, w3_h,
+    ct_h, st_h,
     feat_ref, box_ref,
     q_v, wq, wkv, wo, wqkv, swo, up, down, w1, w2, w3,
-    gat, cnt, kac, vac, kas, vas, qc_v, x1_v, hn_v, hn_o, qs_v, sc_v,
+    mask_s, ct_s, st_s, mem_v, gat, cnt, kac, vac, kas, vas, qc_v, x1_v, hn_v, hn_o, qs_v, sc_v,
     in_sem, gsend, grecv, csend, crecv, hsend, hrecv, msem,
 ):
     n, width = q_v.shape
@@ -106,8 +107,14 @@
     each(n_row - 1, greet)
     pl.semaphore_signal(barrier, inc=1, device_id={"col": other}, device_id_type=MESH)
 
-    mine = pltpu.make_async_copy(mem_hbm, gat.at[row, :, pl.ds(0, width)], msem)
-    mine.start()
+    small = [
+        pltpu.make_async_copy(a, b, msem.at[i])
+        for i, (a, b) in enumerate(
+            ((mem_hbm, mem_v), (mask_h, mask_s), (ct_h, ct_s), (st_h, st_s))
+        )
+    ]
+    for load in small:
+        load.start()
     pairs = (
         (q_hbm, q_v), (wq_h, wq), (wkv_h, wkv), (wo_h, wo), (wqkv_h, wqkv),
         (swo_h, swo), (up_h, up), (down_h, down), (w1_h, w1), (w2_h, w2), (w3_h, w3),
@@ -116,14 +123,18 @@
     for load in loads:
         load.start()
 
-    slot = lax.broadcasted_iota(jnp.int32, (m_dev, LANES), 0)
-    flags = jnp.zeros((m_dev, LANES), jnp.int32)
+    for load in small:
+        load.wait()
+    slot = lax.broadcasted_iota(jnp.int32, (m_dev, width), 0)
+    flags = jnp.zeros((m_dev, width), jnp.int32)
     for i in range(m_dev):
         flags = jnp.where(slot == i, mask_s[i], flags)
-    gat[row, :, pl.ds(width, LANES)] = (flags > 0).astype(F32).astype(BF)
+    gat[row] = jnp.where(flags > 0, mem_v[...].astype(F32), DEAD).astype(BF)
     count = cnt_s[0]
     cnt[0] = jnp.full((8, LANES), count, jnp.int32)
-    mine.wait()
+    loads[0].wait()
+    loads[1].wait()
+    qc_v[...] = mm(rms_round(q_v[...].astype(F32)), wq[...]).astype(BF)
     pl.semaphore_wait(barrier, n_row)
 
     def gather_copy(i):
@@ -140,9 +151,6 @@
     )
     count_copy.start()
 
-    loads[0].wait()
-    loads[1].wait()
-    qc_v[...] = mm(rms_round(q_v[...].astype(F32)), wq[...]).astype(BF)
     loads[2].wait()
 
     def arrived(i):
@@ -156,9 +164,9 @@
     each(n_row - 1, arrived)
 
     keys = n_row * m_dev
-    held = gat[...].reshape(keys, width + LANES)
-    kv = mm(held[:, :width], wkv[...])
-    live = held[:, width:].astype(F32) > 0.0
+    held = gat[...].reshape(keys, width)
+    kv = mm(held, wkv[...])
+    live = held[:, :LANES].astype(F32) < 0.5 * DEAD
     put_keys(kac, vac, pl.ds(0, keys), kv[:, :width], kv[:, width:], live, kv[0:1, :width])
 
     cross_row = scale_row(ct_s, width, hsize)
@@ -242,8 +250,7 @@
     heads = args[14].shape[0]
     keys = n_row * m_dev
     groups = width // LANES
-    tm = min(128, n)
-    smem = pl.BlockSpec(memory_space=pltpu.SMEM)
+    tm = min(256, n)
     hbm = pl.BlockSpec(memory_space=pltpu.HBM)
     vmem = pl.BlockSpec(memory_space=pltpu.VMEM)
     dma = pltpu.SemaphoreType.DMA
@@ -254,12 +261,16 @@
             jax.ShapeDtypeStruct((n, width), F32),
             jax.ShapeDtypeStruct((boxes, n), F32),
         ),
-        in_specs=[hbm, smem, hbm, smem] + [hbm] * 10 + [smem, smem],
+        in_specs=[hbm, pl.BlockSpec(memory_space=pltpu.SMEM)] + [hbm] * 14,
         out_specs=(vmem, vmem),
         scratch_shapes=[pltpu.VMEM(queries.shape, BF)]
         + [pltpu.VMEM(w.shape, BF) for w in weights]
         + [
-            pltpu.VMEM((n_row, m_dev, width + LANES), BF),
+            pltpu.SMEM(mem_mask.shape, jnp.int32),
+            pltpu.SMEM((heads,), F32),
+            pltpu.SMEM((heads,), F32),
+            pltpu.VMEM(memory.shape, BF),
+            pltpu.VMEM((n_row, m_dev, width), BF),
             pltpu.VMEM((2, 8, LANES), jnp.int32),
             pltpu.VMEM((groups, keys, 2 * LANES), BF),
             pltpu.VMEM((groups, keys, 2 * LANES), BF),
@@ -278,13 +289,13 @@
             dma,
             dma((n // tm,)),
             dma((n // tm,)),
-            dma,
+            dma((4,)),
         ],
         compiler_params=pltpu.CompilerParams(
             collective_id=0, has_side_effects=True, vmem_limit_bytes=52 * 1024 * 1024
         ),
         name="spotter",
-    )(pin(queries), counts, pin(memory), mem_mask, *map(pin, weights), *args[14:])
+    )(pin(queries), counts, *map(pin, args[2:4] + weights + args[14:]))
 
 
 def solution(mesh):

time: 29.3 us -> 26 us (0.89)
  Pallas kernels: 25.7 us -> 23.1 us
  local copies, waits for them, and re-layouts: 2.06 us -> 1.39 us
    pallas_call x1, Pallas kernels: 25.7 us -> 23.1 us  [local(): pl.pallas_call(functools.partial(kernel, n_row, width // heads, tm), out_...]
    unnamed x8 -> x2, local copies, waits for them, and re-layouts: 2.06 us -> 1.39 us
where the time goes in v3:
time: 26 us; the launch traced here: 25.8 us
  Pallas kernels  23.1 us (89%)
  local copies, waits for them, and re-layouts  1.39 us (5%)
  between operations  1.29 us (5%)
    pallas_call x1, Pallas kernels, local(): pl.pallas_call(functools.partial(kernel, n_row, width // heads, tm), out_...  23.1 us
    unnamed x2, local copies, waits for them, and re-layouts  1.39 us

profile of v3, /device:TPU:1, one launch (start us, length us, event | category | flops | bytes accessed | tf_op | source)
XLA Modules:
  0.0 25.8 jit_solution(4946424261440971736)
XLA Ops:
  1.3 23.1 %spotter.1 = (f32[512,256]{1,0:T(8,128)S(1)}, f32[4,512]{1,0:T(4,128)S(1)}) custom-call(bf16[512,256]{1,0:T(8,128)(2,1)} %q_hbm.1, s32[1]{0:T(128)S(6)} %copy.20.cnt_s, bf16[16,256]{1,0:T(8,128)(2,1)} %mem_hbm.1, s32[16]{0:T(128)} %mask_h.1, bf16[256,256]{1,0:T(8,128)(2,1)} %wq_h.1, bf16[256,512]{1,0:T(8,128)(2,1)} %wkv_h.1, bf16[256,256]{1,0:T(8,128)(2,1)} %wo_h.1, ...), custom_call_target="tpu_custom_call" | custom-call | tf_op jit(solution)/shard_map/spotter/pallas_call | solution.py:258
  24.4 0.8 %copy.21 = f32[512,256]{1,0:T(8,128)} copy(f32[512,256]{1,0:T(8,128)S(1)} %get-tuple-element.4) | data formatting | bytes 1048576
  25.2 0.6 %copy.22 = f32[4,512]{1,0:T(4,128)} copy(f32[4,512]{1,0:T(4,128)S(1)} %get-tuple-element.5) | data formatting | bytes 16384

commit v4 on v3

--- a/solution.py
+++ b/solution.py
@@ -40,7 +40,7 @@
     return row * (math.log2(math.e) / math.sqrt(hsize))
 
 
-def attend(q, row, ka_ref, va_ref, hsize):
+def attend(q, row, ka_ref, va_ref, keys, hsize):
     rows, width = q.shape
     per = LANES // hsize
     qf = q.astype(F32) * row
@@ -60,9 +60,9 @@
             ],
             axis=0,
         )
-        s = lax.dot_general(lhs, ka_ref[g], (((1,), (1,)), ((), ())), preferred_element_type=F32)
+        s = lax.dot_general(lhs, ka_ref[g, :keys], (((1,), (1,)), ((), ())), preferred_element_type=F32)
         e = jnp.exp2(s - jnp.max(s, axis=-1, keepdims=True)).astype(BF)
-        o = mm(e, va_ref[g])
+        o = mm(e, va_ref[g, :keys])
         num, den = o[:rows, :LANES], o[:rows, LANES:]
         for h in range(1, per):
             part = o[h * rows : (h + 1) * rows]
@@ -83,13 +83,12 @@
         va_ref[g, rows, LANES:] = flags
 
 
-def kernel(
+def mixer(
     n_row, hsize, tm,
-    q_hbm, cnt_s, mem_hbm, mask_h, wq_h, wkv_h, wo_h, wqkv_h, swo_h, up_h, down_h, w1_h, w2_h, w3_h,
-    ct_h, st_h,
-    feat_ref, box_ref,
-    q_v, wq, wkv, wo, wqkv, swo, up, down, w1, w2, w3,
-    mask_s, ct_s, st_s, mem_v, gat, cnt, kac, vac, kas, vas, qc_v, x1_v, hn_v, hn_o, qs_v, sc_v,
+    q_hbm, cnt_s, mem_hbm, mask_h, wq_h, wkv_h, wo_h, wqkv_h, swo_h, up_h, down_h, w1_h, w2_h, w3_h, ct_h, st_h,
+    x1_v, qs_v, kas, vas, cnt, self_row, swo, up, down, w1, w2, w3,
+    q_v, wq, wkv, wo, wqkv,
+    mask_s, ct_s, st_s, mem_v, gat, kac, vac, qc_v, hn_v, hn_o,
     in_sem, gsend, grecv, csend, crecv, hsend, hrecv, msem,
 ):
     n, width = q_v.shape
@@ -135,6 +134,7 @@
     loads[0].wait()
     loads[1].wait()
     qc_v[...] = mm(rms_round(q_v[...].astype(F32)), wq[...]).astype(BF)
+    self_row[...] = scale_row(st_s, width, hsize)
     pl.semaphore_wait(barrier, n_row)
 
     def gather_copy(i):
@@ -182,7 +182,7 @@
 
     def cross_tile(t, carry):
         rows = pl.ds(pl.multiple_of(t * tm, tm), tm)
-        ctx = attend(qc_v[rows, :], cross_row, kac, vac, hsize)
+        ctx = attend(qc_v[rows, :], cross_row, kac, vac, keys, hsize)
         alive = lax.broadcasted_iota(jnp.int32, (tm, width), 0) + t * tm < count
         ctx = jnp.where(alive, ctx, 0.0).astype(BF)
         x1 = q_v[rows, :].astype(F32) + mm(ctx, wo[...])
@@ -205,19 +205,35 @@
     kv_o = mm(hn_o[...], wqkv[:, width:])
     put_keys(kas, vas, pl.ds(n, n), kv_o[:, :width], kv_o[:, width:], spot < cnt[1, 0:1, :], first)
 
-    self_row = scale_row(st_s, width, hsize)
-
-    def self_tile(t, carry):
-        rows = pl.ds(pl.multiple_of(t * tm, tm), tm)
-        sctx = attend(qs_v[rows, :], self_row, kas, vas, hsize)
-        alive = lax.broadcasted_iota(jnp.int32, (tm, width), 0) + t * tm < count
-        sc_v[rows, :] = jnp.where(alive, sctx, 0.0).astype(BF)
-        return carry
-
-    lax.fori_loop(0, n // tm, self_tile, 0)
-
     for load in loads[5:]:
         load.wait()
+    each(n_row - 1, lambda i: gather_copy(i).wait_send())
+
+
+def reader(
+    hsize, tm,
+    x1_v, qs_v, kas, vas, cnt, self_row, swo, up, down, w1, w2, w3,
+    feat_ref, box_ref,
+    sc_v, out_v, box_v, sems,
+):
+    n, width = x1_v.shape
+    count = jnp.max(cnt[0])
+    theirs = jnp.max(cnt[1])
+    sc_v[...] = jnp.zeros_like(sc_v)
+    unit = min(LANES, n)
+    for i in range(n // unit):
+
+        @pl.when((theirs - 1) // unit == i)
+        def _():
+            def self_tile(t, carry):
+                rows = pl.ds(pl.multiple_of(t * tm, tm), tm)
+                sctx = attend(qs_v[rows, :], self_row[...], kas, vas, n + (i + 1) * unit, hsize)
+                alive = lax.broadcasted_iota(jnp.int32, (tm, width), 0) + t * tm < count
+                sc_v[rows, :] = jnp.where(alive, sctx, 0.0).astype(BF)
+                return carry
+
+            lax.fori_loop(0, (count + tm - 1) // tm, self_tile, 0)
+
     x2 = x1_v[...] + mm(sc_v[...], swo[...])
     hn2 = rms_round(x2)
     ff = up.shape[1]
@@ -227,15 +243,19 @@
         upper = jnp.maximum(mm(hn2, up[:, f : f + step]), 0.0).astype(BF)
         x3 = x3 + mm(upper, down[f : f + step, :])
     alive = lax.broadcasted_iota(jnp.int32, (n, width), 0) < count
-    feat_ref[...] = jnp.where(alive, x3, 0.0)
+    out_v[...] = jnp.where(alive, x3, 0.0)
+    put = pltpu.make_async_copy(out_v, feat_ref, sems.at[0])
+    put.start()
     hn3 = rms_round(x3)
     b1 = jnp.maximum(mm(hn3, w1[...]), 0.0).astype(BF)
     b2 = jnp.maximum(mm(b1, w2[...]), 0.0).astype(BF)
     z = lax.dot_general(w3[...], b2, (((1,), (1,)), ((), ())), preferred_element_type=F32)
     box = 1.0 / (1.0 + jnp.exp(-z))
-    box_ref[...] = jnp.where(lax.broadcasted_iota(jnp.int32, box.shape, 1) < count, box, 0.0)
-
-    each(n_row - 1, lambda i: gather_copy(i).wait_send())
+    box_v[...] = jnp.where(lax.broadcasted_iota(jnp.int32, box.shape, 1) < count, box, 0.0)
+    put_box = pltpu.make_async_copy(box_v, box_ref, sems.at[1])
+    put_box.start()
+    put.wait()
+    put_box.wait()
 
 
 def pin(x):
@@ -252,33 +272,34 @@
     groups = width // LANES
     tm = min(256, n)
     hbm = pl.BlockSpec(memory_space=pltpu.HBM)
+    smem = pl.BlockSpec(memory_space=pltpu.SMEM)
     vmem = pl.BlockSpec(memory_space=pltpu.VMEM)
     dma = pltpu.SemaphoreType.DMA
     boxes = weights[-1].shape[0]
-    return pl.pallas_call(
-        functools.partial(kernel, n_row, width // heads, tm),
+    like = jax.ShapeDtypeStruct
+    held = pl.pallas_call(
+        functools.partial(mixer, n_row, width // heads, tm),
         out_shape=(
-            jax.ShapeDtypeStruct((n, width), F32),
-            jax.ShapeDtypeStruct((boxes, n), F32),
-        ),
-        in_specs=[hbm, pl.BlockSpec(memory_space=pltpu.SMEM)] + [hbm] * 14,
-        out_specs=(vmem, vmem),
+            like((n, width), F32),
+            like((n, width), BF),
+            like((groups, 2 * n, 2 * LANES), BF),
+            like((groups, 2 * n, 2 * LANES), BF),
+            like((2, 8, LANES), jnp.int32),
+            like((1, width), F32),
+        )
+        + tuple(like(w.shape, BF) for w in weights[4:]),
+        in_specs=[hbm, smem] + [hbm] * 14,
+        out_specs=(vmem,) * (6 + len(weights[4:])),
         scratch_shapes=[pltpu.VMEM(queries.shape, BF)]
-        + [pltpu.VMEM(w.shape, BF) for w in weights]
+        + [pltpu.VMEM(w.shape, BF) for w in weights[:4]]
         + [
             pltpu.SMEM(mem_mask.shape, jnp.int32),
             pltpu.SMEM((heads,), F32),
             pltpu.SMEM((heads,), F32),
             pltpu.VMEM(memory.shape, BF),
             pltpu.VMEM((n_row, m_dev, width), BF),
-            pltpu.VMEM((2, 8, LANES), jnp.int32),
             pltpu.VMEM((groups, keys, 2 * LANES), BF),
             pltpu.VMEM((groups, keys, 2 * LANES), BF),
-            pltpu.VMEM((groups, 2 * n, 2 * LANES), BF),
-            pltpu.VMEM((groups, 2 * n, 2 * LANES), BF),
-            pltpu.VMEM((n, width), BF),
-            pltpu.VMEM((n, width), F32),
-            pltpu.VMEM((n, width), BF),
             pltpu.VMEM((n, width), BF),
             pltpu.VMEM((n, width), BF),
             pltpu.VMEM((n, width), BF),
@@ -292,10 +313,24 @@
             dma((4,)),
         ],
         compiler_params=pltpu.CompilerParams(
-            collective_id=0, has_side_effects=True, vmem_limit_bytes=52 * 1024 * 1024
+            collective_id=0, has_side_effects=True, vmem_limit_bytes=32 * 1024 * 1024
         ),
-        name="spotter",
+        name="mixer",
     )(pin(queries), counts, *map(pin, args[2:4] + weights + args[14:]))
+    return pl.pallas_call(
+        functools.partial(reader, width // heads, tm),
+        out_shape=(like((n, width), F32), like((boxes, n), F32)),
+        in_specs=[vmem] * 12,
+        out_specs=(hbm, hbm),
+        scratch_shapes=[
+            pltpu.VMEM((n, width), BF),
+            pltpu.VMEM((n, width), F32),
+            pltpu.VMEM((boxes, n), F32),
+            dma((2,)),
+        ],
+        compiler_params=pltpu.CompilerParams(vmem_limit_bytes=32 * 1024 * 1024),
+        name="reader",
+    )(*held)
 
 
 def solution(mesh):

time: 26 us -> 24.6 us (0.946)
  the two profiles are of different devices: /device:TPU:1 before, /device:TPU:4 now
where the time goes in v4:
time: 24.6 us; the launch traced here: 24.4 us
  Pallas kernels  23 us (93%)
  between operations  1.47 us (6%)
    pallas_call x1, Pallas kernels, local(): pl.pallas_call(functools.partial(mixer, n_row, width // heads, tm), out_s...  12.6 us
    pallas_call x1, Pallas kernels, local(): pl.pallas_call(functools.partial(reader, width // heads, tm), out_shape=(...  10.4 us

profile of v4, /device:TPU:4, one launch (start us, length us, event | category | flops | bytes accessed | tf_op | source)
XLA Modules:
  0.0 24.4 jit_solution(9621329138618145567)
XLA Ops:
  1.3 12.6 %mixer.1 = (f32[512,256]{1,0:T(8,128)S(1)}, bf16[512,256]{1,0:T(8,128)(2,1)S(1)}, bf16[2,1024,256]{2,1,0:T(8,128)(2,1)S(1)}, bf16[2,1024,256]{2,1,0:T(8,128)(2,1...) custom-call(bf16[512,256]{1,0:T(8,128)(2,1)} %q_hbm.1, ...), custom_call_target="tpu_custom_call" | custom-call | tf_op jit(solution)/shard_map/mixer/pallas_call | solution.py:280
  13.9 10.4 %reader.1 = (f32[512,256]{1,0:T(8,128)}, f32[4,512]{1,0:T(4,128)}) custom-call(f32[512,256]{1,0:T(8,128)S(1)} %get-tuple-element.14.x1_v, bf16[512,256]{1,0:T(8,128)(2,1)S(1)} %get-tuple-element.15.qs_v, bf16[2,1024,256]{2,1,0:T(8,128)(2,1)S(1)} %get-tuple-element.16.kas, bf16[2,1024,256]{2,1,0:T(8,128)(2,1)S(1)} %get-tuple-element.17.vas, ...), custom_call_target="tpu_custom_call" | custom-call | tf_op jit(solution)/shard_map/reader/pallas_call | solution.py:320

commit v5 on v4

--- a/solution.py
+++ b/solution.py
@@ -318,7 +318,7 @@
         name="mixer",
     )(pin(queries), counts, *map(pin, args[2:4] + weights + args[14:]))
     return pl.pallas_call(
-        functools.partial(reader, width // heads, tm),
+        functools.partial(reader, width // heads, min(512, n)),
         out_shape=(like((n, width), F32), like((boxes, n), F32)),
         in_specs=[vmem] * 12,
         out_specs=(hbm, hbm),

time: 24.6 us -> 26.1 us (1.061)
  the two profiles are of different devices: /device:TPU:4 before, /device:TPU:1 now
where the time goes in v5:
time: 26.1 us; the launch traced here: 26 us
  Pallas kernels  24.5 us (94%)
  between operations  1.51 us (6%)
    pallas_call x1, Pallas kernels, local(): pl.pallas_call(functools.partial(mixer, n_row, width // heads, tm), out_s...  13.9 us
    pallas_call x1, Pallas kernels, local(): pl.pallas_call(functools.partial(reader, width // heads, min(512, n)), ou...  10.5 us

profile of v5, /device:TPU:1, one launch (start us, length us, event | category | flops | bytes accessed | tf_op | source)
XLA Modules:
  0.0 26.0 jit_solution(11895343701193239310)
XLA Ops:
  1.3 13.9 %mixer.1 = (f32[512,256]{1,0:T(8,128)S(1)}, bf16[512,256]{1,0:T(8,128)(2,1)S(1)}, bf16[2,1024,256]{2,1,0:T(8,128)(2,1)S(1)}, bf16[2,1024,256]{2,1,0:T(8,128)(2,1...) custom-call(bf16[512,256]{1,0:T(8,128)(2,1)} %q_hbm.1, ...), custom_call_target="tpu_custom_call" | custom-call | tf_op jit(solution)/shard_map/mixer/pallas_call | solution.py:280
  15.2 10.5 %reader.1 = (f32[512,256]{1,0:T(8,128)}, f32[4,512]{1,0:T(4,128)}) custom-call(f32[512,256]{1,0:T(8,128)S(1)} %get-tuple-element.14.x1_v, bf16[512,256]{1,0:T(8,128)(2,1)S(1)} %get-tuple-element.15.qs_v, bf16[2,1024,256]{2,1,0:T(8,128)(2,1)S(1)} %get-tuple-element.16.kas, bf16[2,1024,256]{2,1,0:T(8,128)(2,1)S(1)} %get-tuple-element.17.vas, ...), custom_call_target="tpu_custom_call" | custom-call | tf_op jit(solution)/shard_map/reader/pallas_call | solution.py:320
